TPU v7x, 256 devices: a whole 4x4x8 slice. The times are simulated.
256 devices in a mesh: dp: 4 (over x), expert: 64 (over z, y, core).
Axes of the slice: x: 4, y: 4, z: 8, core: 2. Of those that a mesh axis runs over, the one named last changes fastest.
Arguments:
- tokens: bfloat16 [4096, 3584], P('expert'), may hold values from -6 to 6
- expert_ids: int32 [4096, 8], P('expert'), may hold values from 0 to 63, all different within a row; in each aligned block of 64 rows (0 to 63, 64 to 127, ...) at most 8 rows name the same one
- weight_num: int32 [4096, 8], P('expert'), may hold values from 64 to 1023
- gate_proj: bfloat16 [64, 3584, 2048], P('expert', None, 'dp'), may hold values from -0.09375 to 0.09375
- up_proj: bfloat16 [64, 3584, 2048], P('expert', None, 'dp'), may hold values from -0.09375 to 0.09375
- down_proj: bfloat16 [64, 2048, 3584], P('expert', 'dp'), may hold values from -0.125 to 0.125
Outputs:
- combined: bfloat16 [4096, 3584], P('expert', 'dp')
Inputs may be any that keep to these rules, and one draw needn't show every extreme that they name: `expert_ids`: in the 64 rows of one device no expert is named by more than 8 rows, and some device has an expert named by exactly 8 of its rows.
All inputs are finite; a program needn't handle non-finite values.
Results may differ from a plain program's by a relative error of at most 0.015.
Values may be sent and summed in bfloat16 or wider, within the bound.
A program may use at most 192 MiB of HBM per device.

v0:
```python
import jax
import jax.numpy as jnp
from jax import lax
from jax.sharding import PartitionSpec as P

ROOM = 8


def slot_matrices(ids, num, experts, capacity):
    rows = ids.shape[0]
    slots = experts * capacity
    column = jnp.arange(slots, dtype=jnp.int32)[None, :]
    expert_of = column // capacity
    hits = [ids[:, k : k + 1] == expert_of for k in range(ids.shape[1])]
    named = sum((h.astype(jnp.float32) for h in hits))
    weight = sum((jnp.where(h, num[:, k : k + 1], 0) for k, h in enumerate(hits)))
    earlier = jnp.arange(rows)[:, None] > jnp.arange(rows)[None, :]
    position = jnp.dot(
        earlier.astype(jnp.bfloat16), named.astype(jnp.bfloat16), preferred_element_type=jnp.float32
    )
    here = (named > 0) & (position == (column % capacity).astype(jnp.float32))
    high = jnp.where(here, weight // 32 * 32, 0).astype(jnp.bfloat16)
    low = jnp.where(here, weight % 32, 0).astype(jnp.bfloat16)
    return (here.astype(jnp.bfloat16), high, low)


def local(tokens, expert_ids, weight_num, gate_proj, up_proj, down_proj):
    experts = lax.axis_size("expert")
    parts = lax.axis_size("dp")
    width = tokens.shape[1]
    quarter = width // parts
    slots = experts * ROOM
    here, high, low = slot_matrices(expert_ids, weight_num, experts, ROOM)
    mine = lax.dynamic_slice_in_dim(tokens, lax.axis_index("dp") * quarter, quarter, 1)
    outgoing = lax.dot_general(
        here, mine, (((0,), (0,)), ((), ())), preferred_element_type=jnp.float32
    ).astype(jnp.bfloat16)
    arrived = lax.all_to_all(
        outgoing.reshape(experts, ROOM, quarter), "expert", split_axis=0, concat_axis=0, tiled=True
    ).reshape(slots, quarter)
    rows = lax.all_gather(arrived, "dp", axis=0, tiled=True)
    gate_out, up_out = (0.0, 0.0)
    for q in range(parts):
        block = rows[q * slots : (q + 1) * slots]
        cut = slice(q * quarter, (q + 1) * quarter)
        gate_out += jnp.dot(block, gate_proj[0, cut], preferred_element_type=jnp.float32)
        up_out += jnp.dot(block, up_proj[0, cut], preferred_element_type=jnp.float32)
    hidden = (jax.nn.silu(gate_out) * up_out).astype(jnp.bfloat16)
    partial = jnp.concatenate(
        [
            jnp.dot(
                hidden,
                down_proj[0, :, q * quarter : (q + 1) * quarter],
                preferred_element_type=jnp.float32,
            ).astype(jnp.bfloat16)
            for q in range(parts)
        ],
        axis=0,
    )
    summed = lax.psum_scatter(partial, "dp", scatter_dimension=0, tiled=True)
    returned = lax.all_to_all(
        summed.reshape(experts, ROOM, quarter), "expert", split_axis=0, concat_axis=0, tiled=True
    ).reshape(slots, quarter)
    total = jnp.dot(high, returned, preferred_element_type=jnp.float32)
    total += jnp.dot(low, returned, preferred_element_type=jnp.float32)
    return (total / 1024.0).astype(jnp.bfloat16)


def solution(mesh):
    placed = (
        P("expert", None),
        P("expert", None),
        P("expert", None),
        P("expert", None, "dp"),
        P("expert", None, "dp"),
        P("expert", "dp", None),
    )
    return jax.shard_map(
        local, mesh=mesh, in_specs=placed, out_specs=P("expert", "dp"), check_vma=False
    )
```

profile of v0, /device:TPU:1, one launch (start us, length us, event | category | flops | bytes accessed | tf_op | source)
XLA Modules:
  0.0 203.0 jit_solution(10615380470221626891)
XLA Ops:
  6.5 0.0 copy-start
  6.5 0.0 all-gather.2.cloned.1.call-start
  6.5 1.0 slice_bitcast_fusion.15
  7.5 0.3 fusion.5
  7.9 0.0 copy-done
  7.9 0.5 fusion.1
  8.3 38.4 %all_to_all.10 = bf16[64,8,896]{2,1,0:T(8,128)(2,1)} all-to-all(bf16[64,8,896]{2,1,0:T(8,128)(2,1)S(1)} %fusion.1), channel_id=1, replica_groups=mesh['dp'=4,'expert'=64] {'expert'}, dimensions={0} | all-to-all | bytes 1835008 | tf_op jit(solution)/shard_map/all_to_all | solution.py:38
  46.7 0.0 all-gather.2.cloned.1.call-update
  46.7 0.0 reduce-scatter.2.cloned.1.call-start
  46.8 43.6 %all-gather.2.cloned.1.call-done = bf16[2048,896]{1,0:T(8,128)(2,1)} async-done(((bf16[512,896]{1,0:T(8,128)(2,1)}), bf16[2048,896]{1,0:T(8,128)(2,1)}) %all-gather.2.cloned.1.call-update) | async-done | bytes 3670032 | tf_op jit(solution)/shard_map/all_gather | solution.py:41
  90.4 0.0 copy-start.1
  90.4 0.0 copy-start.2
  90.4 2.3 %fusion.21 = f32[512,512]{1,0:T(8,128)S(1)} fusion(bf16[1,3584,512]{2,1,0:T(8,128)(2,1)} %param.9, bf16[2048,896]{1,0:T(8,128)(2,1)} %all-gather.2.cloned.1.call-done), kind=kOutput, calls=%fused_computation.35 | convolution fusion | flops 469762048 | bytes 2883584 | tf_op jit(solution)/shard_map/dot_general | solution.py:46
  92.7 2.5 %convolution_add_fusion.5 = f32[512,512]{1,0:T(8,128)S(1)} fusion(f32[512,512]{1,0:T(8,128)S(1)} %fusion.21, bf16[1,3584,512]{2,1,0:T(8,128)(2,1)} %param.9, bf16[2048,896]{1,0:T(8,128)(2,1)} %all-gather.2.cloned.1.call-done), kind=kOutput, calls=%fused_computation.12 | convolution fusion | flops 470024192 | bytes 3932160 | tf_op jit(solution)/shard_map/dot_general | solution.py:46
  95.3 0.0 copy-done.1
  95.3 0.0 copy-done.2
  95.3 0.0 copy-start.3
  95.3 0.7 convolution_add_fusion.4
  96.0 0.7 convolution_add_fusion.3
  96.7 0.6 copy-done.3
  97.3 0.7 fusion.16
  98.0 0.7 convolution_add_fusion.2
  98.7 0.7 convolution_add_fusion.1
  99.5 0.0 copy-start.5
  99.5 0.8 fusion.2
  100.3 1.2 copy-done.5
  101.5 0.7 convolution_convert_fusion.1
  102.2 0.7 convolution_convert_fusion.2
  102.9 0.7 convolution_convert_fusion.3
  103.7 0.7 convolution_convert_fusion.4
  104.4 8.7 %pad_maximum_fusion = bf16[2048,896]{1,0:T(8,128)(2,1)} fusion(bf16[512,896]{1,0:T(8,128)(2,1)S(1)} %convolution_convert_fusion.1, bf16[512,896]{1,0:T(8,128)(2,1)S(1)} %convolution_convert_fusion.2, bf16[512,896]{1,0:T(8,128)(2,1)S(1)} %convolution_convert_fusion.3, bf16[512,896]{1,0:T(8,128)(2,1)S(1)} %convolution_convert_fusion.4), kind=kLoop, calls=%fused_computation | loop fusion | flops 14680064 | bytes 7340032 | tf_op jit(solution)/shard_map/concatenate | solution.py:49
  113.1 0.0 copy-start.4
  113.1 0.0 reduce-scatter.2.cloned.1.call-update
  113.1 45.6 %reduce-scatter.2.cloned.1.call-done = bf16[512,896]{1,0:T(8,128)(2,1)} async-done(((bf16[2048,896]{1,0:T(8,128)(2,1)}), bf16[512,896]{1,0:T(8,128)(2,1)}) %reduce-scatter.2.cloned.1.call-update) | async-done | bytes 917520 | tf_op jit(solution)/shard_map/reduce_scatter | solution.py:60
  158.7 10.6 %all-to-all-start.1 = ((bf16[64,8,896]{2,1,0:T(8,128)(2,1)}), bf16[64,8,896]{2,1,0:T(8,128)(2,1)S(1)}, u32[]{:S(2)}, u32[]{:S(2)}) async-start(bf16[64,8,896]{2,1,0:T(8,128)(2,1)} %bitcast.83), calls=%async_computation.2 | async-start | bytes 1835008 | tf_op jit(solution)/shard_map/all_to_all | solution.py:61
  169.3 0.0 copy-done.4
  169.4 25.3 %all-to-all-done.1 = bf16[64,8,896]{2,1,0:T(8,128)(2,1)S(1)} async-done(((bf16[64,8,896]{2,1,0:T(8,128)(2,1)}), bf16[64,8,896]{2,1,0:T(8,128)(2,1)S(1)}, u32[]{:S(2)}, u32[]{:S(2)}) %all-to-all-start.1) | async-done | bytes 917536 | tf_op jit(solution)/shard_map/all_to_all | solution.py:61
  194.6 0.5 fusion.7
  195.1 1.1 fusion.4
  (2 shorter events, 0.0 us)
Async XLA Ops:
  6.5 1.3 copy-start
  6.5 83.9 %all-gather.2.cloned.1.call-start = ((), (), s32[]{:S(2)}) async-start(), calls=%async_computation.3 | async-start | bytes 4587520 | tf_op jit(solution)/shard_map/all_gather | solution.py:41
  46.7 112.0 %reduce-scatter.2.cloned.1.call-start = ((), (), s32[]{:S(2)}) async-start(), calls=%async_computation.4 | async-start | bytes 4587520 | tf_op jit(solution)/shard_map/reduce_scatter | solution.py:60
  90.4 4.9 %copy-start.1 = (bf16[2048,896]{1,0:T(8,128)(2,1)S(1)}, bf16[2048,896]{1,0:T(8,128)(2,1)}, u32[]{:S(2)}) copy-start(bf16[2048,896]{1,0:T(8,128)(2,1)} %all-gather.2.cloned.1.call-done) | copy-start | bytes 11010052
  90.4 4.9 %copy-start.2 = (bf16[1,3584,512]{2,1,0:T(8,128)(2,1)S(1)}, bf16[1,3584,512]{2,1,0:T(8,128)(2,1)}, u32[]{:S(2)}) copy-start(bf16[1,3584,512]{2,1,0:T(8,128)(2,1)} %param.9) | copy-start | bytes 11010052
  95.3 2.0 %copy-start.3 = (bf16[1,3584,512]{2,1,0:T(8,128)(2,1)S(1)}, bf16[1,3584,512]{2,1,0:T(8,128)(2,1)}, u32[]{:S(2)}) copy-start(bf16[1,3584,512]{2,1,0:T(8,128)(2,1)} %param.10) | copy-start | bytes 11010052
  99.5 2.0 %copy-start.5 = (bf16[1,512,3584]{2,1,0:T(8,128)(2,1)S(1)}, bf16[1,512,3584]{2,1,0:T(8,128)(2,1)}, u32[]{:S(2)}) copy-start(bf16[1,512,3584]{2,1,0:T(8,128)(2,1)} %param.11) | copy-start | bytes 11010052
  113.1 56.2 %copy-start.4 = (s32[64,8]{0,1:T(8,128)S(1)}, s32[64,8]{0,1:T(8,128)}, u32[]{:S(2)}) copy-start(s32[64,8]{0,1:T(8,128)} %param.8) | copy-start | bytes 6148
  158.7 35.9 %all-to-all-start.1 = ((bf16[64,8,896]{2,1,0:T(8,128)(2,1)}), bf16[64,8,896]{2,1,0:T(8,128)(2,1)S(1)}, u32[]{:S(2)}, u32[]{:S(2)}) async-start(bf16[64,8,896]{2,1,0:T(8,128)(2,1)} %bitcast.83), calls=%async_computation.2 | async-start | bytes 1835008 | tf_op jit(solution)/shard_map/all_to_all | solution.py:61
Sparse Core Ops, SparseCore 0:
  46.8 43.5 all-gather.1
  113.2 45.3 reduce-scatter.1
where the time goes:
time: 203 us
  waiting for transfers between devices  115 us (57%)
  blocking collectives  38.4 us (19%)
  matrix products  14.4 us (7%)
  between operations  13.6 us (7%)
  starting transfers between devices  10.7 us (5%)
  other arithmetic  8.73 us (4%)
  local copies, waits for them, and re-layouts  2.81 us (1%)
    reduce_scatter x1, waiting for transfers between devices, local(): summed = lax.psum_scatter(partial, 'dp', scatter_dimension=0, tiled=True)  45.6 us
    all_gather x1, waiting for transfers between devices, local(): rows = lax.all_gather(arrived, 'dp', axis=0, tiled=True)  43.6 us
    all_to_all x1, blocking collectives, local(): lax.all_to_all(outgoing.reshape(experts, ROOM, quarter), 'expert', split_...  38.4 us
    all_to_all x1, waiting for transfers between devices, local(): lax.all_to_all(summed.reshape(experts, ROOM, quarter), 'expert', split_ax...  25.3 us
    all_to_all x1, starting transfers between devices, local(): lax.all_to_all(summed.reshape(experts, ROOM, quarter), 'expert', split_ax...  10.6 us
    concatenate x1, other arithmetic, local(): jnp.concatenate([jnp.dot(hidden, down_proj[0, :, q * quarter:(q + 1) * qu...  8.72 us
    dot_general x4, matrix products, local(): jnp.dot(block, gate_proj[0, cut], preferred_element_type=jnp.float32)  6.26 us
  transfers between devices with their start and end apart: 3, of which 3 were waited for; matrix products, arithmetic and copies ran while one was open for 0% of the time, Pallas kernels for 0%

commit v1 on v0

--- a/solution.py
+++ b/solution.py
@@ -4,6 +4,13 @@
 from jax.sharding import PartitionSpec as P
 
 ROOM = 8
+
+
+def gather_over(block, mesh_axis, dim):
+    size = lax.axis_size(mesh_axis)
+    tiles = jnp.stack([block for _ in range(size)])
+    tiles = lax.all_to_all(tiles, mesh_axis, split_axis=0, concat_axis=0)
+    return jnp.concatenate(tiles, axis=dim)
 
 
 def slot_matrices(ids, num, experts, capacity):
@@ -38,7 +45,7 @@
     arrived = lax.all_to_all(
         outgoing.reshape(experts, ROOM, quarter), "expert", split_axis=0, concat_axis=0, tiled=True
     ).reshape(slots, quarter)
-    rows = lax.all_gather(arrived, "dp", axis=0, tiled=True)
+    rows = gather_over(arrived, "dp", 0)
     gate_out, up_out = (0.0, 0.0)
     for q in range(parts):
         block = rows[q * slots : (q + 1) * slots]

time: 203 us -> 199 us (0.980)
  waiting for transfers between devices: 115 us -> 67.5 us
  blocking collectives: 38.4 us -> 83.9 us
  matrix products: 14.4 us -> 10.9 us
    all_to_all x0 -> x1, blocking collectives: none -> 45.6 us  [gather_over(): tiles = lax.all_to_all(tiles, mesh_axis, split_axis=0, concat_axis=0)]
    all_gather x1 -> x0, waiting for transfers between devices: 43.6 us -> none  [local(): rows = lax.all_gather(arrived, 'dp', axis=0, tiled=True)]
    dot_general x4, matrix products: 6.26 us -> 2.82 us  [local(): jnp.dot(block, gate_proj[0, cut], preferred_element_type=jnp.float32)]
    reduce_scatter x1, waiting for transfers between devices: 45.6 us -> 42.2 us  [local(): summed = lax.psum_scatter(partial, 'dp', scatter_dimension=0, tiled=True)]
  transfers between devices with their start and end apart: 3 -> 2, of which waited for: 3 -> 2; matrix products, arithmetic and copies ran while one was open for 0% -> 0% of each run, Pallas kernels for 0% -> 0%
where the time goes in v1:
time: 199 us; the launch traced here: 198 us
  blocking collectives  83.9 us (42%)
  waiting for transfers between devices  67.5 us (34%)
  between operations  13.6 us (7%)
  matrix products  10.9 us (5%)
  starting transfers between devices  10.6 us (5%)
  other arithmetic  8.73 us (4%)
  local copies, waits for them, and re-layouts  3.08 us (2%)
    all_to_all x1, blocking collectives, gather_over(): tiles = lax.all_to_all(tiles, mesh_axis, split_axis=0, concat_axis=0)  45.6 us
    reduce_scatter x1, waiting for transfers between devices, local(): summed = lax.psum_scatter(partial, 'dp', scatter_dimension=0, tiled=True)  42.2 us
    all_to_all x1, blocking collectives, local(): lax.all_to_all(outgoing.reshape(experts, ROOM, quarter), 'expert', split_...  38.3 us
    all_to_all x1, waiting for transfers between devices, local(): lax.all_to_all(summed.reshape(experts, ROOM, quarter), 'expert', split_ax...  25.3 us
    all_to_all x1, starting transfers between devices, local(): lax.all_to_all(summed.reshape(experts, ROOM, quarter), 'expert', split_ax...  10.6 us
    concatenate x1, other arithmetic, local(): jnp.concatenate([jnp.dot(hidden, down_proj[0, :, q * quarter:(q + 1) * qu...  8.73 us
  transfers between devices with their start and end apart: 2, of which 2 were waited for; matrix products, arithmetic and copies ran while one was open for 0% of the time, Pallas kernels for 0%

profile of v1, /device:TPU:1, one launch (start us, length us, event | category | flops | bytes accessed | tf_op | source)
XLA Modules:
  0.0 198.3 jit_solution(8852733025367053792)
XLA Ops:
  6.5 0.0 copy-start
  6.5 0.0 reduce-scatter.2.cloned.1.call-start
  6.5 1.0 slice_bitcast_fusion.27
  7.5 0.3 fusion.5
  7.9 0.0 copy-done
  7.9 0.5 fusion.1
  8.3 38.3 %all_to_all.15 = bf16[64,8,896]{2,1,0:T(8,128)(2,1)S(1)} all-to-all(bf16[64,8,896]{2,1,0:T(8,128)(2,1)S(1)} %fusion.1), channel_id=1, replica_groups=mesh['dp'=4,'expert'=64] {'expert'}, dimensions={0} | all-to-all | bytes 1835008 | tf_op jit(solution)/shard_map/all_to_all | solution.py:45
  46.6 0.3 stack.3
  46.9 0.0 copy-start.1
  46.9 45.6 %all_to_all.16 = bf16[4,512,896]{2,1,0:T(8,128)(2,1)S(1)} all-to-all(bf16[4,512,896]{2,1,0:T(8,128)(2,1)S(1)} %stack.3), channel_id=1, replica_groups=mesh['dp'=4,'expert'=64] {'dp'}, dimensions={0} | all-to-all | bytes 7340032 | tf_op jit(solution)/shard_map/all_to_all | solution.py:12
  92.5 0.0 copy-done.1
  92.5 0.7 fusion.21
  93.2 0.7 convolution_add_fusion.5
  93.9 0.0 copy-start.2
  94.0 0.7 convolution_add_fusion.4
  94.7 0.7 convolution_add_fusion.3
  95.4 0.6 copy-done.2
  96.0 0.7 fusion.16
  96.7 0.7 convolution_add_fusion.2
  97.4 0.7 convolution_add_fusion.1
  98.1 0.0 copy-start.4
  98.1 0.8 fusion.2
  99.0 1.2 copy-done.4
  100.2 0.7 convolution_convert_fusion.1
  100.9 0.7 convolution_convert_fusion.2
  101.6 0.7 convolution_convert_fusion.3
  102.3 0.7 convolution_convert_fusion.4
  103.0 8.7 %pad_maximum_fusion = bf16[2048,896]{1,0:T(8,128)(2,1)} fusion(bf16[512,896]{1,0:T(8,128)(2,1)S(1)} %convolution_convert_fusion.1, bf16[512,896]{1,0:T(8,128)(2,1)S(1)} %convolution_convert_fusion.2, bf16[512,896]{1,0:T(8,128)(2,1)S(1)} %convolution_convert_fusion.3, bf16[512,896]{1,0:T(8,128)(2,1)S(1)} %convolution_convert_fusion.4), kind=kLoop, calls=%fused_computation | loop fusion | flops 14680064 | bytes 7340032 | tf_op jit(solution)/shard_map/concatenate | solution.py:56
  111.7 0.0 copy-start.3
  111.7 0.0 reduce-scatter.2.cloned.1.call-update
  111.8 42.2 %reduce-scatter.2.cloned.1.call-done = bf16[512,896]{1,0:T(8,128)(2,1)} async-done(((bf16[2048,896]{1,0:T(8,128)(2,1)}), bf16[512,896]{1,0:T(8,128)(2,1)}) %reduce-scatter.2.cloned.1.call-update) | async-done | bytes 917520 | tf_op jit(solution)/shard_map/reduce_scatter | solution.py:67
  154.0 10.6 %all-to-all-start.2 = ((bf16[64,8,896]{2,1,0:T(8,128)(2,1)}), bf16[64,8,896]{2,1,0:T(8,128)(2,1)S(1)}, u32[]{:S(2)}, u32[]{:S(2)}) async-start(bf16[64,8,896]{2,1,0:T(8,128)(2,1)} %bitcast.99), calls=%async_computation.3 | async-start | bytes 1835008 | tf_op jit(solution)/shard_map/all_to_all | solution.py:68
  164.6 0.0 copy-done.3
  164.6 25.3 %all-to-all-done.2 = bf16[64,8,896]{2,1,0:T(8,128)(2,1)S(1)} async-done(((bf16[64,8,896]{2,1,0:T(8,128)(2,1)}), bf16[64,8,896]{2,1,0:T(8,128)(2,1)S(1)}, u32[]{:S(2)}, u32[]{:S(2)}) %all-to-all-start.2) | async-done | bytes 917536 | tf_op jit(solution)/shard_map/all_to_all | solution.py:68
  189.9 0.5 fusion.7
  190.4 1.1 fusion.4
  (2 shorter events, 0.0 us)
Async XLA Ops:
  6.5 1.3 copy-start
  6.5 147.4 %reduce-scatter.2.cloned.1.call-start = ((), (), s32[]{:S(2)}) async-start(), calls=%async_computation.4 | async-start | bytes 4587520 | tf_op jit(solution)/shard_map/reduce_scatter | solution.py:67
  46.9 45.7 %copy-start.1 = (bf16[1,3584,512]{2,1,0:T(8,128)(2,1)S(1)}, bf16[1,3584,512]{2,1,0:T(8,128)(2,1)}, u32[]{:S(2)}) copy-start(bf16[1,3584,512]{2,1,0:T(8,128)(2,1)} %param.9) | copy-start | bytes 11010052
  93.9 2.0 %copy-start.2 = (bf16[1,3584,512]{2,1,0:T(8,128)(2,1)S(1)}, bf16[1,3584,512]{2,1,0:T(8,128)(2,1)}, u32[]{:S(2)}) copy-start(bf16[1,3584,512]{2,1,0:T(8,128)(2,1)} %param.10) | copy-start | bytes 11010052
  98.1 2.0 %copy-start.4 = (bf16[1,512,3584]{2,1,0:T(8,128)(2,1)S(1)}, bf16[1,512,3584]{2,1,0:T(8,128)(2,1)}, u32[]{:S(2)}) copy-start(bf16[1,512,3584]{2,1,0:T(8,128)(2,1)} %param.11) | copy-start | bytes 11010052
  111.7 52.9 %copy-start.3 = (s32[64,8]{0,1:T(8,128)S(1)}, s32[64,8]{0,1:T(8,128)}, u32[]{:S(2)}) copy-start(s32[64,8]{0,1:T(8,128)} %param.8) | copy-start | bytes 6148
  154.0 35.9 %all-to-all-start.2 = ((bf16[64,8,896]{2,1,0:T(8,128)(2,1)}), bf16[64,8,896]{2,1,0:T(8,128)(2,1)S(1)}, u32[]{:S(2)}, u32[]{:S(2)}) async-start(bf16[64,8,896]{2,1,0:T(8,128)(2,1)} %bitcast.99), calls=%async_computation.3 | async-start | bytes 1835008 | tf_op jit(solution)/shard_map/all_to_all | solution.py:68
Sparse Core Ops, SparseCore 0:
  111.9 42.0 reduce-scatter.1
